TPU v7x, 32 devices: a whole 2x2x4 slice. The times are simulated.
32 devices in a mesh: ctx: 8 (over z, y), head: 4 (over x, core).
Axes of the slice: x: 2, y: 2, z: 4, core: 2. Of those that a mesh axis runs over, the one named last changes fastest.
Arguments:
- tokens: bfloat16 [4096, 1024], P('ctx'), may hold values from -24 to 24
- w_query: bfloat16 [1024, 1024], P(None, 'head'), may hold values from -0.1875 to 0.1875
- w_key: bfloat16 [1024, 1024], P(None, 'head'), may hold values from -0.1875 to 0.1875
- w_value: bfloat16 [1024, 1024], P(None, 'head'), may hold values from -0.1875 to 0.1875
- w_out: bfloat16 [1024, 1024], P('head'), may hold values from -0.1875 to 0.1875
- block_mask: int32 [32, 32], replicated, may hold values from 0 to 1, as said below
- block_order: int32 [32], replicated, may hold values from 0 to 31, each once
Outputs:
- mixed: bfloat16 [4096, 1024], P('ctx', 'head')
Inputs may be any that keep to these rules, and one draw needn't show every extreme that they name: `block_mask`: entries are 0 or 1 and every diagonal entry is 1. `block_order`: each initial block index appears once.
All inputs are finite; a program needn't handle non-finite values.
Results may differ from a plain program's by a relative error of at most 0.013.
Values may be sent and summed in bfloat16 or wider, within the bound.
No kernel may reach another device: no remote copies, remote signals or barrier semaphores. Data moves between devices by JAX's collectives and lax.ppermute only.
A program may use at most 256 MiB of HBM per device.

v0:
```python
import jax
import jax.numpy as jnp
from jax import lax
from jax.sharding import PartitionSpec as P

HEAD_DIM = 64
BLOCK = 128


def body(tokens, w_query, w_key, w_value, w_out, block_mask, block_order):
    tok_rows = tokens.shape[0]
    features = w_query.shape[1]
    heads_here = features // HEAD_DIM
    query_proj = jnp.dot(tokens, w_query, preferred_element_type=jnp.float32).astype(jnp.bfloat16)
    key_proj = jnp.dot(tokens, w_key, preferred_element_type=jnp.float32).astype(jnp.bfloat16)
    value_proj = jnp.dot(tokens, w_value, preferred_element_type=jnp.float32).astype(jnp.bfloat16)
    query_heads = query_proj.reshape(tok_rows, heads_here, HEAD_DIM)
    position = lax.axis_index("ctx")
    blocks_here = tok_rows // BLOCK
    own_order = lax.dynamic_slice_in_dim(block_order, position * blocks_here, blocks_here)
    mask_rows = jnp.take(block_mask, own_order, axis=0)
    scale = HEAD_DIM ** (-0.5)
    running = (
        jnp.full((heads_here, tok_rows), -1e30, jnp.float32),
        jnp.zeros((heads_here, tok_rows), jnp.float32),
        jnp.zeros((tok_rows, heads_here, HEAD_DIM), jnp.float32),
    )
    kv_pair = jnp.stack([key_proj, value_proj])
    kv_piece = lax.all_gather(kv_pair, "ctx", axis=1, tiled=True)
    key_piece = kv_piece[0]
    key_blocks = jnp.arange(key_piece.shape[0], dtype=jnp.int32) // BLOCK
    key_orig = jnp.take(block_order, key_blocks)
    block_cols = jnp.take(mask_rows, key_orig, axis=1)
    allowed = jnp.repeat(block_cols, BLOCK, axis=0) > 0
    row_max, row_sum, weighted = running
    count = key_piece.shape[0]
    key_heads = key_piece.reshape(count, heads_here, HEAD_DIM)
    value_heads = kv_piece[1].reshape(count, heads_here, HEAD_DIM)
    scores = (
        jnp.einsum("qhd,khd->hqk", query_heads, key_heads, preferred_element_type=jnp.float32)
        * scale
    )
    tile_max = jnp.max(jnp.where(allowed[None], scores, -1e30), axis=2)
    new_max = jnp.maximum(row_max, tile_max)
    probs = jnp.where(allowed[None], jnp.exp(scores - new_max[:, :, None]), 0.0)
    row_sum = jnp.sum(probs, axis=2)
    partial_value = jnp.einsum(
        "hqk,khd->qhd", probs.astype(jnp.bfloat16), value_heads, preferred_element_type=jnp.float32
    )
    weighted = partial_value
    running = (new_max, row_sum, weighted)
    row_max, row_sum, weighted = running
    attended = (
        (weighted / jnp.transpose(row_sum)[:, :, None])
        .astype(jnp.bfloat16)
        .reshape(tok_rows, features)
    )
    partial_out = jnp.dot(attended, w_out, preferred_element_type=jnp.float32)
    return lax.psum_scatter(
        partial_out.astype(jnp.bfloat16), "head", scatter_dimension=1, tiled=True
    )


def solution(mesh):
    placed = (
        P("ctx", None),
        P(None, "head"),
        P(None, "head"),
        P(None, "head"),
        P("head", None),
        P(),
        P(),
    )
    return jax.shard_map(
        body, mesh=mesh, in_specs=placed, out_specs=P("ctx", "head"), check_vma=False
    )
```

profile of v0, /device:TPU:0, one launch (start us, length us, event | category | flops | bytes accessed | tf_op | source)
XLA Modules:
  0.0 177.6 jit_solution(7759355805128871058)
XLA Ops:
  6.5 0.0 copy-start
  6.5 0.0 all-gather.2.cloned.1.call-start
  6.5 1.2 copy-done
  7.8 1.5 fusion.9
  9.2 1.5 fusion.10
  10.7 0.8 pad_maximum_fusion
  11.6 0.0 all-gather.2.cloned.1.call-update
  11.6 0.0 reduce-scatter.2.cloned.1.call-start
  11.6 0.7 compare_and_fusion.1
  12.4 1.3 gather_fusion
  13.7 0.1 broadcast_select_fusion
  13.7 0.1 copy.13
  13.9 0.1 compare_reduce_fusion.23
  13.9 0.1 compare_reduce_fusion.22
  14.0 0.1 compare_reduce_fusion.21
  14.1 0.1 compare_reduce_fusion.20
  14.1 0.1 compare_reduce_fusion.19
  14.2 0.1 compare_reduce_fusion.18
  14.2 0.1 compare_reduce_fusion.17
  14.3 0.1 compare_reduce_fusion.16
  14.3 0.1 compare_reduce_fusion.15
  14.4 0.1 compare_reduce_fusion.14
  14.5 0.1 compare_reduce_fusion.13
  14.5 0.1 compare_reduce_fusion.12
  14.6 0.1 compare_reduce_fusion.11
  14.6 0.1 compare_reduce_fusion.10
  14.7 0.1 compare_reduce_fusion.9
  14.8 0.1 compare_reduce_fusion.8
  14.8 0.1 compare_reduce_fusion.7
  14.9 0.1 compare_reduce_fusion.6
  14.9 0.1 compare_reduce_fusion.5
  15.0 0.1 compare_reduce_fusion.4
  15.0 0.1 compare_reduce_fusion.3
  15.1 0.1 compare_reduce_fusion.2
  15.2 0.1 compare_reduce_fusion.1
  15.2 0.1 compare_reduce_fusion
  15.3 1.8 %fusion.27 = (s32[1]{0:T(128)}, s32[1]{0:T(128)}, s32[1]{0:T(128)}, s32[1]{0:T(128)}, s32[1]{0:T(128)}, /*index=5*/s32[1]{0:T(128)}, s32[1]{0:T(128)}, s32[1]{0:...) fusion(s32[32]{0:T(128)} %param.13), kind=kLoop, calls=%fused_computation.82 | loop fusion | bytes 104 | tf_op jit(solution)/shard_map/jit(_take)/gather | solution.py:32
  17.1 2.1 %fusion.26 = (s32[1]{0:T(128)}, s32[1]{0:T(128)}, s32[1]{0:T(128)}, s32[1]{0:T(128)}, s32[1]{0:T(128)}, /*index=5*/s32[1]{0:T(128)}, s32[1]{0:T(128)}, s32[1]{0:...) fusion(s32[32]{0:T(128)} %param.13), kind=kLoop, calls=%fused_computation.81 | loop fusion | bytes 152 | tf_op jit(solution)/shard_map/jit(_take)/gather | solution.py:32
  19.2 4.5 %compare_select_fusion.2 = s32[4096,1]{0,1:T(1,128)S(1)} fusion(s32[]{:T(128)} %bitcast.28, s32[]{:T(128)} %bitcast.29, s32[]{:T(128)} %bitcast.30, s32[]{:T(128)} %bitcast.31, s32[]{:T(128)} %bitcast.32, s32[]{:T(128)} %bitcast.34, s32[]{:T(128)} %bitcast.33), kind=kLoop, calls=%fused_computation.47 | loop fusion | flops 94208 | bytes 16412 | tf_op jit(solution)/shard_map/jit(_take)/gather | solution.py:32
  23.7 15.5 %compare_and_fusion = (pred[4096]{0:T(1024)(128)(4,1)S(1)}, s32[4096]{0:T(1024)S(1)}) fusion(pred[4096]{0:T(1024)(128)(4,1)S(1)} %compare_reduce_fusion, pred[4096]{0:T(1024)(128)(4,1)S(1)} %compare_reduce_fusion.1, pred[4096]{0:T(1024)(128)(4,1)S(1)} %compare_reduce_fusion.2, pred[4096]{0:T(1024)(128)(4,1)S(1)} %compare_reduce_fusion.3, ...), kind=kLoop, calls=%fused_computation.71 | loop fusion | flops 188416 | bytes 139364 | tf_op jit(solution)/shard_map/jit(_take)/and | solution.py:33
  39.3 10.8 %gather_fusion.1 = s32[4096,4]{1,0:T(8,128)S(1)} fusion(s32[4,32]{0,1:T(8,128)S(1)} %copy.13, s32[4096]{0:T(1024)S(1)} %broadcast_clamp_fusion), kind=kCustom, calls=%fused_computation.1 | custom fusion | bytes 147456 | tf_op jit(solution)/shard_map/jit(_take)/gather | solution.py:33
  50.0 2.8 %fusion.5 = pred[4,4096]{0,1:T(8,128)(4,1)} fusion(s32[4096,4]{1,0:T(8,128)S(1)} %gather_fusion.1, pred[4096]{0:T(1024)(128)(4,1)S(1)} %get-tuple-element.5), kind=kLoop, calls=%fused_computation.9 | loop fusion | flops 32768 | bytes 86016 | tf_op jit(solution)/shard_map/gt | solution.py:34
  52.9 1.7 copy.14
  54.6 1.5 convolution_convert_fusion.1
  56.1 31.1 %all-gather.2.cloned.1.call-done = bf16[2,4096,256]{2,1,0:T(8,128)(2,1)} async-done(((bf16[2,512,256]{2,1,0:T(8,128)(2,1)}), bf16[2,4096,256]{2,1,0:T(8,128)(2,1)}) %all-gather.2.cloned.1.call-update) | async-done | bytes 4194320 | tf_op jit(solution)/shard_map/all_gather | solution.py:29
  87.2 3.8 %fusion.25 = (bf16[1,4096,256]{2,1,0:T(8,128)(2,1)}, bf16[1,4096,256]{2,1,0:T(8,128)(2,1)S(1)}) fusion(bf16[2,4096,256]{2,1,0:T(8,128)(2,1)} %all-gather.2.cloned.1.call-done), kind=kLoop, calls=%fused_computation.80 | loop fusion | bytes 8388608 | tf_op jit(solution)/shard_map/slice | solution.py:30
  91.1 4.1 %copy.15 = bf16[1,4096,256]{1,2,0:T(8,128)(2,1)} copy(bf16[1,4096,256]{2,1,0:T(8,128)(2,1)} %get-tuple-element.9) | data formatting | bytes 4194304 | tf_op jit(solution)/shard_map/slice | solution.py:30
  95.2 3.0 %copy.12 = bf16[1,4096,256]{1,2,0:T(8,128)(2,1)} copy(bf16[1,4096,256]{2,1,0:T(8,128)(2,1)S(1)} %get-tuple-element.10) | data formatting | bytes 4194304 | tf_op jit(solution)/shard_map/slice | solution.py:38
  98.1 0.9 broadcast_in_dim.65
  99.0 15.8 %select_reduce_fusion = (f32[4,512]{1,0:T(4,128)S(1)}, f32[4,512,4096]{2,1,0:T(8,128)}) fusion(pred[512,4096]{1,0:T(8,128)(4,1)S(1)} %bitcast.64, bf16[512,4,64]{0,2,1:T(8,128)(2,1)S(1)} %bitcast.69, bf16[4096,4,64]{0,2,1:T(8,128)(2,1)} %bitcast.68), kind=kOutput, calls=%fused_computation.3 | convolution fusion | flops 1098905600 | bytes 38019072 | tf_op jit(solution)/shard_map/qhd,khd->hqk/dot_general | solution.py:40
  114.8 15.2 %fusion = f32[4,512]{1,0:T(4,128)S(1)} fusion(f32[4,512,4096]{2,1,0:T(8,128)} %get-tuple-element.44, f32[4,512]{1,0:T(4,128)S(1)} %broadcast_maximum_fusion, pred[512,4096]{1,0:T(8,128)(4,1)S(1)} %bitcast.65), kind=kLoop, calls=%fused_computation.4 | loop fusion | flops 33552384 | bytes 35667968 | tf_op jit(solution)/shard_map/reduce_sum | solution.py:46
  130.0 14.7 %fusion.14 = bf16[512,4,64]{0,2,1:T(8,128)(2,1)S(1)} fusion(bf16[4096,4,64]{0,2,1:T(8,128)(2,1)} %bitcast.67, f32[4,512,4096]{2,1,0:T(8,128)} %get-tuple-element.44, f32[4,512]{1,0:T(4,128)S(1)} %broadcast_maximum_fusion, pred[512,4096]{1,0:T(8,128)(4,1)S(1)} %bitcast.66, f32[512,4]{0,1:T(4,128)S(1)} %bitcast.74), kind=kOutput, calls=%fused_computation.18 | convolution fusion | flops 1107558400 | bytes 38027264 | tf_op jit(solution)/shard_map/hqk,khd->qhd/dot_general | solution.py:47
  144.7 2.5 %convolution_convert_fusion = bf16[512,1024]{1,0:T(8,128)(2,1)} fusion(bf16[512,256]{0,1:T(8,128)(2,1)S(1)} %bitcast.70, bf16[256,1024]{1,0:T(8,128)(2,1)} %param.11), kind=kOutput, calls=%fused_computation.10 | convolution fusion | flops 268959744 | bytes 1835008 | tf_op jit(solution)/shard_map/dot_general | solution.py:58
  147.2 0.0 reduce-scatter.2.cloned.1.call-update
  147.2 23.5 %reduce-scatter.2.cloned.1.call-done = bf16[512,256]{1,0:T(8,128)(2,1)} async-done(((bf16[512,1024]{1,0:T(8,128)(2,1)}), bf16[512,256]{1,0:T(8,128)(2,1)}) %reduce-scatter.2.cloned.1.call-update) | async-done | bytes 262160 | tf_op jit(solution)/shard_map/reduce_scatter | solution.py:59
  (5 shorter events, 0.1 us)
Async XLA Ops:
  6.5 1.2 copy-start
  6.5 80.7 %all-gather.2.cloned.1.call-start = ((), (), s32[]{:S(2)}) async-start(), calls=%async_computation.1 | async-start | bytes 4718592 | tf_op jit(solution)/shard_map/all_gather | solution.py:29
  11.6 159.1 %reduce-scatter.2.cloned.1.call-start = ((), (), s32[]{:S(2)}) async-start(), calls=%async_computation.2 | async-start | bytes 1310720 | tf_op jit(solution)/shard_map/reduce_scatter | solution.py:59
Sparse Core Ops, SparseCore 0:
  11.7 75.4 all-gather.1
  147.4 23.3 reduce-scatter.1
where the time goes:
time: 179 us; the launch traced here: 178 us
  waiting for transfers between devices  54.7 us (31%)
  other arithmetic  41.2 us (23%)
  matrix products  37.4 us (21%)
  local copies, waits for them, and re-layouts  30.7 us (17%)
  between operations  13.5 us (8%)
    all_gather x1, waiting for transfers between devices, body(): kv_piece = lax.all_gather(kv_pair, 'ctx', axis=1, tiled=True)  31.1 us
    reduce_scatter x1, waiting for transfers between devices, body(): lax.psum_scatter(partial_out.astype(jnp.bfloat16), 'head', scatter_dimens...  23.5 us
    dot_general x1, matrix products, body(): jnp.einsum('qhd,khd->hqk', query_heads, key_heads, preferred_element_type...  15.8 us
    and x1, other arithmetic, body(): block_cols = jnp.take(mask_rows, key_orig, axis=1)  15.5 us
    reduce_sum x1, other arithmetic, body(): row_sum = jnp.sum(probs, axis=2)  15.2 us
    dot_general x1, matrix products, body(): jnp.einsum('hqk,khd->qhd', probs.astype(jnp.bfloat16), value_heads, prefe...  14.7 us
    gather x1, local copies, waits for them, and re-layouts, body(): block_cols = jnp.take(mask_rows, key_orig, axis=1)  10.8 us
    slice x2, local copies, waits for them, and re-layouts, body(): key_piece = kv_piece[0]  7.92 us
  transfers between devices with their start and end apart: 2, of which 2 were waited for; matrix products, arithmetic and copies ran while one was open for 25% of the time, Pallas kernels for 0%

commit v1 on v0

v1 whole, which is shorter than its diff:
```python
import functools

import jax
import jax.numpy as jnp
from jax import lax
from jax.experimental import pallas as pl
from jax.experimental.pallas import tpu as pltpu
from jax.sharding import PartitionSpec as P


HEAD_DIM = 64
BLOCK = 128
LANES = 128
PAIR = 2
SLOTS = 4
LINES = 2
TALL = HEAD_DIM + 16
NEG = -1e30


HBM = pl.BlockSpec(memory_space=pltpu.HBM)
VMEM = pl.BlockSpec(memory_space=pltpu.VMEM)
SMEM = pl.BlockSpec(memory_space=pltpu.SMEM)
GRANT = 16 * 1024 * 1024
WHOLE = 60 * 1024 * 1024


def proj_kernel(inner, tok_in, wk_in, wv_in, wq_in, *rest):
    outs, (tok, wk, wv, wq, msg, sems) = rest[:4], rest[4:]
    loads = [
        pltpu.make_async_copy(src, dst, sems.at[n])
        for n, (src, dst) in enumerate(((tok_in, tok), (wv_in, wv), (wk_in, wk), (wq_in, wq)))
    ]
    for load in loads:
        load.start()
    low = (lax.axis_index("ctx") // inner) % PAIR
    rows = tok.shape[0]
    loads[0].wait()
    loads[1].wait()
    v = jnp.dot(tok[...], wv[...], preferred_element_type=jnp.float32)
    loads[2].wait()
    loads[3].wait()
    q = jnp.dot(tok[...], wq[...], preferred_element_type=jnp.float32) * HEAD_DIM ** (-0.5)
    k = jnp.dot(tok[...], wk[...], preferred_element_type=jnp.float32)
    for g in range(PAIR):
        cols = slice(g * LANES, (g + 1) * LANES)
        msg[g, :rows] = k[:, cols].astype(jnp.bfloat16)
        for base, x in ((rows, v), (2 * rows, q)):
            for i in range(rows // BLOCK):
                block = x[i * BLOCK : (i + 1) * BLOCK, cols]
                start = base + i * BLOCK
                msg[g, start : start + BLOCK] = jnp.transpose(block).astype(jnp.bfloat16)
    for j, out in enumerate(outs):
        out[...] = msg[low ^ (j % PAIR), : out.shape[0]]


def list_kernel(inner, outer, per, cap, mask, order, who, where, which, valid, first, steps, names, ends, load):
    c = lax.axis_index("ctx")
    a = c // inner
    b = (c % inner) // 2 * 2 + lax.axis_index("head") % 2
    part_blocks = inner * PAIR * per
    parts = outer // PAIR
    size = PAIR * per
    span = part_blocks + SLOTS

    def name(dev, _):
        kb = ((lax.div(dev, inner) ^ a) * inner + (lax.rem(dev, inner) ^ b)) * per
        for i in range(per):
            names[dev * per + i] = order[kb + i]
        return 0

    lax.fori_loop(0, inner * outer, name, 0)

    def piece(n, _):
        part, k = lax.div(n, PAIR), lax.rem(n, PAIR)
        qb = ((k ^ a) * inner + b) * per
        own = [order[qb + i] for i in range(per)]

        def col(m, to):
            to = list(to)
            for e in range(8):
                slot = m * 8 + e
                key = names[part * part_blocks + slot]
                for i in range(per):
                    which[to[i]] = slot
                    to[i] = to[i] + mask[own[i], key]
            return tuple(to)

        begin = [(n * per + i) * span for i in range(per)]
        end = lax.fori_loop(0, part_blocks // 8, col, tuple(begin))
        for i in range(per):
            some = end[i] > begin[i]
            keep = jnp.where(some, which[begin[i]], 0)
            for extra in range(SLOTS):
                which[end[i] + extra] = keep
            ends[n * per + i] = end[i]
        return 0

    lax.fori_loop(0, parts * PAIR, piece, 0)
    for part in range(parts):
        for s in range(LINES):
            load[s] = 0

        def row(qi, _):
            s, least = jnp.int32(0), load[0]
            for other in range(1, LINES):
                here = load[other]
                s = jnp.where(here < least, other, s)
                least = jnp.minimum(here, least)
            item = (part * LINES + s) * cap + least
            start = (part * size + qi) * span
            count = ends[part * size + qi] - start
            items = lax.div(count + (SLOTS - 1), SLOTS)
            first[item] = 1

            def mark(t, left):
                who[item + t] = qi
                where[item + t] = start + t * SLOTS
                valid[item + t] = left
                first[item + t + 1] = 0
                return left - SLOTS

            lax.fori_loop(0, items, mark, count)
            load[s] = least + items
            return 0

        lax.fori_loop(0, size, row, 0)
        most = load[0]
        for s in range(1, LINES):
            most = jnp.maximum(most, load[s])
        steps[part] = most
        for s in range(LINES):
            start = (part * LINES + s) * cap
            last = start + jnp.maximum(load[s] - 1, 0)
            idle = load[s] == 0
            qi = jnp.where(idle, size, who[last])
            key = jnp.where(idle, part * size * span, where[last])

            def fill(t, _):
                who[start + t] = qi
                where[start + t] = key
                valid[start + t] = 0
                first[start + t] = 0
                return 0

            lax.fori_loop(load[s], most + 2, fill, 0)


def attend_kernel(part, per, cap, n_kv, n_q, who, where, which, valid, first, steps, *rest):
    ins, rest = rest[:n_kv], rest[n_kv:]
    q_in, rest = rest[:n_q], rest[n_q:]
    if part:
        (acc_old, m_old_all), rest = rest[:2], rest[2:]
        outs, (kq, vt, qt, sc, m_s, al_s, acc_s, acc_all, m_all) = rest[:n_q], rest[n_q:]
    else:
        (acc_all, m_all), (kq, vt, qt, sc, m_s, al_s, acc_s) = rest[:2], rest[2:]
    nq = n_q * per
    rows = per * BLOCK
    zero = jnp.zeros((HEAD_DIM, BLOCK), jnp.bfloat16)
    ones = jnp.ones((TALL - HEAD_DIM, BLOCK), jnp.bfloat16)
    for k, msg in enumerate(q_in):
        for i in range(per):
            start = 2 * rows + i * BLOCK
            turned = msg[start : start + BLOCK, :]
            qt[k * per + i] = jnp.concatenate([turned[:HEAD_DIM], zero], axis=0)
            qt[nq + 1 + k * per + i] = jnp.concatenate([zero, turned[HEAD_DIM:]], axis=0)
    for e in range(PAIR):
        qt[e * (nq + 1) + nq] = jnp.zeros((LANES, BLOCK), jnp.bfloat16)
    for n, msg in enumerate(ins):
        for i in range(per):
            kq[n * per + i] = msg[i * BLOCK : (i + 1) * BLOCK, :]
            start = rows + i * BLOCK
            for e in range(PAIR):
                at = 2 * (n * per + i) + e
                vt[at, :HEAD_DIM] = msg[start + e * HEAD_DIM : start + (e + 1) * HEAD_DIM, :]
                vt[at, HEAD_DIM:] = ones
    m_s[...] = jnp.full(m_s.shape, NEG, jnp.float32)
    acc_s[...] = jnp.zeros(acc_s.shape, jnp.float32)
    if part:
        acc_all[...] = acc_old[...]

    def score(t, buf, s):
        line, e = s // PAIR, s % PAIR
        at = (part * LINES + line) * cap + t
        row = e * (nq + 1) + who[at]
        start = where[at]
        q = qt[row]
        tiles = []
        for f in range(SLOTS):
            tile = jnp.dot(kq[which[start + f]], q, preferred_element_type=jnp.float32)
            sc[buf, s, f] = tile
            tiles.append(tile.reshape(BLOCK // 8, 8, BLOCK))
        top = jnp.max(functools.reduce(jnp.maximum, tiles), axis=0)
        top = jnp.max(top, axis=0, keepdims=True)
        before = m_old_all[row] if part else NEG
        m_old = jnp.where(first[at] == 1, before, m_s[1 - buf, s])
        m_new = jnp.where(valid[at] > 0, jnp.maximum(m_old, top), m_old)
        al_s[buf, s] = jnp.exp(m_old - m_new)
        m_s[buf, s] = m_new

    def weigh(t, buf, s):
        line, e = s // PAIR, s % PAIR
        at = (part * LINES + line) * cap + t
        row = e * (nq + 1) + who[at]
        start = where[at]
        n_valid = valid[at]
        m, alpha = m_s[buf, s], al_s[buf, s]
        acc = acc_s[s]
        if part:
            acc = jnp.where(first[at] == 1, acc_old[row], acc)
        acc = acc * alpha
        for f in range(0, SLOTS, 2):
            probs, values = [], []
            for n in (f, f + 1):
                shut = m + jnp.where(n < n_valid, 0.0, -NEG)
                probs.append(jnp.exp(sc[buf, s, n] - shut).astype(jnp.bfloat16))
                values.append(vt[which[start + n] * 2 + e])
            acc = acc + jnp.dot(
                jnp.concatenate(values, axis=1),
                jnp.concatenate(probs, axis=0),
                preferred_element_type=jnp.float32,
            )
        acc_s[s] = acc
        acc_all[row] = acc
        if not part:
            m_all[row] = m

    streams = range(LINES * PAIR)
    for s in streams:
        score(0, 0, s)
    count = steps[part]

    def step(u, _):
        for buf in (0, 1):
            for s in streams:
                score(2 * u + 1 + buf, 1 - buf, s)
                weigh(2 * u + buf, buf, s)
        return 0

    lax.fori_loop(0, lax.div(count, 2), step, 0)

    @pl.when(lax.rem(count, 2) == 1)
    def _():
        for s in streams:
            weigh(count - 1, 0, s)

    if part:
        for k in range(n_q):
            for i in range(per):
                done = []
                for e in range(PAIR):
                    total = acc_all[e * (nq + 1) + k * per + i]
                    done.append(total[:HEAD_DIM] * (1.0 / total[HEAD_DIM : HEAD_DIM + 1]))
                outs[k][i * BLOCK : (i + 1) * BLOCK, :] = jnp.transpose(
                    jnp.concatenate(done, axis=0)
                ).astype(jnp.bfloat16)


def out_kernel(inner, groups, *refs):
    pieces, ws, out = refs[: groups * PAIR], refs[groups * PAIR : -1], refs[-1]
    low = (lax.axis_index("ctx") // inner) % PAIR
    rows = []
    for g in range(groups):
        for k in range(PAIR):
            start = pl.multiple_of(LANES * (low ^ k), LANES)
            rows.append(ws[g][pl.ds(start, LANES), :])
    x = jnp.concatenate([piece[...] for piece in pieces], axis=1)
    w = jnp.concatenate(rows, axis=0)
    out[...] = jnp.dot(x, w, preferred_element_type=jnp.float32).astype(out.dtype)


def solution(mesh):
    ctx, groups = mesh.shape["ctx"], mesh.shape["head"]

    def body(tokens, w_query, w_key, w_value, w_out, block_mask, block_order):
        rows = tokens.shape[0]
        outer = w_query.shape[1] // HEAD_DIM
        inner = ctx // outer
        per = rows // BLOCK
        nb = block_mask.shape[0]
        nq = PAIR * per
        cols = w_out.shape[1] // groups
        bf, f32 = jnp.bfloat16, jnp.float32
        params = pltpu.CompilerParams(vmem_limit_bytes=GRANT)
        both = ("ctx", "head")
        places = [(c // inner, c % inner, h) for c in range(ctx) for h in range(groups)]

        def index(a, b, h):
            return (a * inner + b) * groups + h

        def turn(x, j, g=0):
            pairs = [
                (index(a, b, h), index(a ^ j, (b & ~1) | (h & 1), ((h & ~1) | (b & 1)) ^ g))
                for a, b, h in places
            ]
            return lax.ppermute(x, both, pairs)

        def spread(x, e):
            pairs = [
                (index(a, b, h), index(a, b ^ (e & ~1), h ^ (e & 1))) for a, b, h in places
            ]
            return lax.ppermute(x, both, pairs) if e else x

        def head_swap(x, j):
            return lax.ppermute(x, "head", [(h, h ^ j) for h in range(groups)]) if j else x

        sizes = [3 * rows] * PAIR + [2 * rows] * (outer - PAIR)
        msgs = pl.pallas_call(
            functools.partial(proj_kernel, inner),
            out_shape=[jax.ShapeDtypeStruct((n, LANES), bf) for n in sizes],
            in_specs=[HBM] * 4,
            out_specs=[VMEM] * len(sizes),
            scratch_shapes=[pltpu.VMEM(x.shape, bf) for x in (tokens, w_value, w_key, w_query)]
            + [
                pltpu.VMEM((PAIR, 3 * rows, LANES), bf),
                pltpu.SemaphoreType.DMA((4,)),
            ],
            compiler_params=pltpu.CompilerParams(vmem_limit_bytes=WHOLE),
            name="proj",
        )(tokens, w_key, w_value, w_query)
        got = [turn(msgs[j], j) for j in range(outer)]
        parts = outer // PAIR
        part_nb = nb // parts
        longest = -(-part_nb // SLOTS)
        cap = -(-nq * longest // LINES) + longest + 3
        table = jax.ShapeDtypeStruct((parts * LINES * cap,), jnp.int32)
        tables = pl.pallas_call(
            functools.partial(list_kernel, inner, outer, per, cap),
            out_shape=[
                table,
                table,
                jax.ShapeDtypeStruct((parts * nq * (part_nb + SLOTS),), jnp.int32),
                table,
                table,
                jax.ShapeDtypeStruct((parts,), jnp.int32),
            ],
            in_specs=[SMEM] * 2,
            out_specs=[SMEM] * 6,
            scratch_shapes=[
                pltpu.SMEM((nb,), jnp.int32),
                pltpu.SMEM((parts * nq,), jnp.int32),
                pltpu.SMEM((LINES,), jnp.int32),
            ],
            name="block_lists",
        )(block_mask, block_order)
        h = lax.axis_index("head")
        w_out, msgs = lax.optimization_barrier((w_out, msgs))
        w_cols = []
        for g in range(groups):
            share = lax.dynamic_slice_in_dim(w_out, (h ^ g) * cols, cols, axis=1)
            w_cols.append(head_swap(share, g))
        got[0], tables = lax.optimization_barrier((got[0], tables))
        wide = PAIR * (nq + 1)
        state = [
            jax.ShapeDtypeStruct((wide, TALL, BLOCK), f32),
            jax.ShapeDtypeStruct((wide, 1, BLOCK), f32),
        ]
        made = []
        for part in range(parts):
            last = part > 0
            pieces = range(part * PAIR, (part + 1) * PAIR)
            if last:
                got[pieces[0]], made = lax.optimization_barrier((got[pieces[0]], made))
            kv = [spread(got[j], e) for j in pieces for e in range(inner)]
            made = pl.pallas_call(
                functools.partial(attend_kernel, part, per, cap, len(kv), PAIR),
                out_shape=[jax.ShapeDtypeStruct((rows, LANES), bf)] * PAIR if last else state,
                in_specs=[SMEM] * 6 + [VMEM] * (len(kv) + PAIR + len(made)),
                out_specs=[VMEM] * 2,
                scratch_shapes=[
                    pltpu.VMEM((part_nb, BLOCK, LANES), bf),
                    pltpu.VMEM((2 * part_nb, TALL, BLOCK), bf),
                    pltpu.VMEM((wide, LANES, BLOCK), bf),
                    pltpu.VMEM((2, LINES * PAIR, SLOTS, BLOCK, BLOCK), f32),
                    pltpu.VMEM((2, LINES * PAIR, 1, BLOCK), f32),
                    pltpu.VMEM((2, LINES * PAIR, 1, BLOCK), f32),
                    pltpu.VMEM((LINES * PAIR, TALL, BLOCK), f32),
                ]
                + ([pltpu.VMEM(x.shape, f32) for x in state] if last else []),
                compiler_params=params,
            )(*tables, *kv, *got[:PAIR], *made)
        pieces = []
        for g in range(0, groups, 2):
            for k in range(PAIR):
                pieces.append(turn(made[k], k, g))
        gathered = []
        for g in range(0, groups, 2):
            own = pieces[g : g + PAIR]
            gathered += own
            gathered += [head_swap(own[k], 1) for k in range(PAIR)]
        return pl.pallas_call(
            functools.partial(out_kernel, inner, groups),
            out_shape=jax.ShapeDtypeStruct((rows, cols), bf),
            in_specs=[VMEM] * (len(gathered) + groups),
            out_specs=VMEM,
            compiler_params=params,
            name="out_proj",
        )(*gathered, *w_cols)

    placed = (
        P("ctx", None),
        P(None, "head"),
        P(None, "head"),
        P(None, "head"),
        P("head", None),
        P(),
        P(),
    )
    return jax.shard_map(
        body, mesh=mesh, in_specs=placed, out_specs=P("ctx", "head"), check_vma=False
    )
```

time: 179 us -> 66.8 us (0.37)
  other arithmetic: 41.2 us -> 0 us
  matrix products: 37.4 us -> 0 us
  waiting for transfers between devices: 54.7 us -> 19.7 us
  starting transfers between devices: 0.04 us -> 32.6 us
  local copies, waits for them, and re-layouts: 30.7 us -> 0.1 us
  Pallas kernels: 0 us -> 14 us
  between operations: 13.5 us -> 0.15 us
    dot_general x6 -> x0, matrix products: 37.4 us -> none  [the longest x1 15.8 us: body(): jnp.einsum('qhd,khd->hqk', query_heads, key_heads, preferred_element_type...]
    ppermute x0 -> x19, starting transfers between devices: none -> 32.6 us  [the longest x8 12.6 us: turn(): return lax.ppermute(x, both, pairs)]
    all_gather x1 -> x0, waiting for transfers between devices: 31.1 us -> none  [body(): kv_piece = lax.all_gather(kv_pair, 'ctx', axis=1, tiled=True)]
    reduce_scatter x1 -> x0, waiting for transfers between devices: 23.5 us -> none  [body(): lax.psum_scatter(partial_out.astype(jnp.bfloat16), 'head', scatter_dimens...]
    ppermute x0 -> x19, waiting for transfers between devices: none -> 19.7 us  [the longest x8 18.7 us: turn(): return lax.ppermute(x, both, pairs)]
    and x2 -> x0, other arithmetic: 16.3 us -> none  [the longest x1 15.5 us: body(): block_cols = jnp.take(mask_rows, key_orig, axis=1)]
    gather x4 -> x0, local copies, waits for them, and re-layouts: 16 us -> none  [the longest x1 10.8 us: body(): block_cols = jnp.take(mask_rows, key_orig, axis=1)]
    reduce_sum x1 -> x0, other arithmetic: 15.2 us -> none  [body(): row_sum = jnp.sum(probs, axis=2)]
  transfers between devices with their start and end apart: 2 -> 19, of which waited for: 2 -> 6; matrix products, arithmetic and copies ran while one was open for 25% -> 0% of each run, Pallas kernels for 0% -> 14%
where the time goes in v1:
time: 66.8 us; the launch traced here: 66.5 us
  starting transfers between devices  32.6 us (49%)
  waiting for transfers between devices  19.7 us (29%)
  Pallas kernels  14 us (21%)
    ppermute x8, waiting for transfers between devices, turn(): return lax.ppermute(x, both, pairs)  18.7 us
    ppermute x8, starting transfers between devices, turn(): return lax.ppermute(x, both, pairs)  12.6 us
    ppermute x7, starting transfers between devices, head_swap(): lax.ppermute(x, 'head', [(h, h ^ j) for h in range(groups)])  10.3 us
    ppermute x4, starting transfers between devices, spread(): return lax.ppermute(x, both, pairs) if e else x  9.64 us
    pallas_call x2, Pallas kernels, body(): pl.pallas_call(functools.partial(attend_kernel, part, per, cap, len(kv),...  6.03 us
    pallas_call x1, Pallas kernels, body(): pl.pallas_call(functools.partial(proj_kernel, inner), out_shape=[jax.Shap...  3.82 us
    pallas_call x1, Pallas kernels, body(): pl.pallas_call(functools.partial(list_kernel, inner, outer, per, cap), ou...  2.96 us
  transfers between devices with their start and end apart: 19, of which 6 were waited for; matrix products, arithmetic and copies ran while one was open for 0% of the time, Pallas kernels for 14%

profile of v1, /device:TPU:0, one launch (start us, length us, event | category | flops | bytes accessed | tf_op | source)
XLA Modules:
  0.0 66.5 jit_solution(7699409465218912242)
XLA Ops:
  0.0 3.8 %proj.1 = (bf16[1536,128]{1,0:T(8,128)(2,1)}, bf16[1536,128]{1,0:T(8,128)(2,1)}, bf16[1024,128]{1,0:T(8,128)(2,1)}, bf16[1024,128]{1,0:T(8,128)(2,1)}) custom-call(bf16[512,1024]{1,0:T(8,128)(2,1)} %tok_in.1, bf16[1024,256]{1,0:T(8,128)(2,1)} %wk_in.1, bf16[1024,256]{1,0:T(8,128)(2,1)} %wv_in.1, bf16[1024,256]{1,0:T(8,128)(2,1)} %wq_in.1), custom_call_target="tpu_custom_call" | custom-call | tf_op jit(solution)/shard_map/proj/pallas_call | solution.py:308
  3.8 1.7 %collective-permute-start = (bf16[1536,128]{1,0:T(8,128)(2,1)}, bf16[1536,128]{1,0:T(8,128)(2,1)S(1)}, u32[]{:S(2)}, u32[]{:S(2)}) collective-permute-start(bf16[1536,128]{1,0:T(8,128)(2,1)} %get-tuple-element.30), channel_id=1, source_target_pairs={{0,0},{1,4},{2,2},{3,6},{4,1},{5,5},{6,3},{7,7},{8,8},{9,12},{10,1... | collective-permute-start | bytes 1179656 | tf_op jit(solution)/shard_map/ppermute | solution.py:296
  5.5 3.1 %collective-permute-start.3 = (bf16[1536,128]{1,0:T(8,128)(2,1)}, bf16[1536,128]{1,0:T(8,128)(2,1)S(1)}, u32[]{:S(2)}, u32[]{:S(2)}) collective-permute-start(bf16[1536,128]{1,0:T(8,128)(2,1)} %get-tuple-element.45), channel_id=1, source_target_pairs={{0,8},{1,12},{2,10},{3,14},{4,9},{5,13},{6,11},{7,15},{8,0},{9,4},... | collective-permute-start | bytes 1179656 | tf_op jit(solution)/shard_map/ppermute | solution.py:296
  8.6 3.0 %block_lists.1 = (s32[92]{0:T(128)}, s32[92]{0:T(128)}, s32[320]{0:T(512)}, s32[92]{0:T(128)}, s32[92]{0:T(128)}, /*index=5*/s32[2]{0:T(128)}) custom-call(s32[32,32]{1,0:T(8,128)} %mask.1, s32[32]{0:T(128)} %order.1), custom_call_target="tpu_custom_call" | custom-call | tf_op jit(solution)/shard_map/block_lists/pallas_call | solution.py:327
  11.5 0.0 collective-permute-done.rest_0_.rest_4_
  11.5 0.0 copy-start.4
  11.6 0.0 copy-start.5
  11.6 0.0 copy-start
  11.6 5.2 %collective-permute-start.2 = (bf16[1536,128]{1,0:T(8,128)(2,1)S(1)}, bf16[1536,128]{1,0:T(8,128)(2,1)S(1)}, u32[]{:S(2)}, u32[]{:S(2)}) collective-permute-start(bf16[1536,128]{1,0:T(8,128)(2,1)S(1)} %collective-permute-done.rest_0_.rest_4_), channel_id=1, source_target_pairs={{0,1},{1,0},{2,3},{3,2},{4,5},{5,4},{6,7},{7,6},{8,9},{9,8},{10,11... | collective-permute-start | bytes 1179656 | tf_op jit(solution)/shard_map/ppermute | solution.py:302
  16.8 0.9 %collective-permute-done.3.rest_2_.rest_5_ = bf16[1536,128]{1,0:T(8,128)(2,1)S(1)} collective-permute-done((bf16[1536,128]{1,0:T(8,128)(2,1)}, bf16[1536,128]{1,0:T(8,128)(2,1)S(1)}, u32[]{:S(2)}, u32[]{:S(2)}) %collective-permute-start.3) | collective-permute-done | bytes 393248 | tf_op jit(solution)/shard_map/ppermute | solution.py:296
  17.7 1.1 %collective-permute-start.4 = (bf16[1536,128]{1,0:T(8,128)(2,1)S(1)}, bf16[1536,128]{1,0:T(8,128)(2,1)S(1)}, u32[]{:S(2)}, u32[]{:S(2)}) collective-permute-start(bf16[1536,128]{1,0:T(8,128)(2,1)S(1)} %collective-permute-done.3.rest_2_.rest_5_), channel_id=1, source_target_pairs={{0,1},{1,0},{2,3},{3,2},{4,5},{5,4},{6,7},{7,6},{8,9},{9,8},{10,11... | collective-permute-start | bytes 1179656 | tf_op jit(solution)/shard_map/ppermute | solution.py:302
  18.8 0.0 copy-start.1
  18.8 0.0 copy-start.2
  18.8 0.0 copy-start.3
  18.8 3.6 %collective-permute-start.6 = (bf16[1024,128]{1,0:T(8,128)(2,1)}, bf16[1024,128]{1,0:T(8,128)(2,1)S(1)}, u32[]{:S(2)}, u32[]{:S(2)}) collective-permute-start(bf16[1024,128]{1,0:T(8,128)(2,1)} %get-tuple-element.49), channel_id=1, source_target_pairs={{0,24},{1,28},{2,26},{3,30},{4,25},{5,29},{6,27},{7,31},{8,16},{9,... | collective-permute-start | bytes 786440 | tf_op jit(solution)/shard_map/ppermute | solution.py:296
  22.4 0.0 copy-start.6
  22.4 0.0 collective-permute-start.1
  22.4 6.7 %collective-permute-done.6.rest_2_ = bf16[1024,128]{1,0:T(8,128)(2,1)S(1)} collective-permute-done((bf16[1024,128]{1,0:T(8,128)(2,1)}, bf16[1024,128]{1,0:T(8,128)(2,1)S(1)}, u32[]{:S(2)}, u32[]{:S(2)}) %collective-permute-start.6) | collective-permute-done | bytes 262176 | tf_op jit(solution)/shard_map/ppermute | solution.py:296
  29.2 1.9 %collective-permute-start.7 = (bf16[1024,128]{1,0:T(8,128)(2,1)S(1)}, bf16[1024,128]{1,0:T(8,128)(2,1)S(1)}, u32[]{:S(2)}, u32[]{:S(2)}) collective-permute-start(bf16[1024,128]{1,0:T(8,128)(2,1)S(1)} %collective-permute-done.6.rest_2_), channel_id=1, source_target_pairs={{0,1},{1,0},{2,3},{3,2},{4,5},{5,4},{6,7},{7,6},{8,9},{9,8},{10,11... | collective-permute-start | bytes 786440 | tf_op jit(solution)/shard_map/ppermute | solution.py:302
  31.1 0.0 collective-permute-done.2.rest_1_
  31.1 0.0 collective-permute-done.4.rest_3_
  31.1 0.0 copy-done.4
  31.1 0.0 copy-done.5
  31.1 0.0 copy-done
  31.1 0.0 copy-done.1
  31.1 0.0 copy-done.2
  31.1 0.0 copy-done.3
  31.1 3.1 %shard_map.73 = (f32[18,80,128]{2,1,0:T(8,128)S(1)}, f32[18,1,128]{2,1,0:T(1,128)S(1)}) custom-call(s32[92]{0:T(128)S(1)} %copy-done.1, s32[92]{0:T(128)S(1)} %copy-done.2, s32[320]{0:T(512)S(1)} %copy-done, s32[92]{0:T(128)S(1)} %copy-done.3, s32[92]{0:T(128)S(1)} %copy-done.4, s32[2]{0:T(128)S(1)} %copy-done.5, ...), custom_call_target="tpu_custom_call" | custom-call | tf_op jit(solution)/shard_map/pallas_call | solution.py:365
  34.2 11.1 %collective-permute-done.1.rest_0_ = bf16[1024,128]{1,0:T(8,128)(2,1)S(1)} collective-permute-done((bf16[1024,128]{1,0:T(8,128)(2,1)}, bf16[1024,128]{1,0:T(8,128)(2,1)S(1)}, u32[]{:S(2)}, u32[]{:S(2)}) %collective-permute-start.1) | collective-permute-done | bytes 262176 | tf_op jit(solution)/shard_map/ppermute | solution.py:296
  45.3 1.4 %collective-permute-start.5 = (bf16[1024,128]{1,0:T(8,128)(2,1)S(1)}, bf16[1024,128]{1,0:T(8,128)(2,1)S(1)}, u32[]{:S(2)}, u32[]{:S(2)}) collective-permute-start(bf16[1024,128]{1,0:T(8,128)(2,1)S(1)} %collective-permute-done.1.rest_0_), channel_id=1, source_target_pairs={{0,1},{1,0},{2,3},{3,2},{4,5},{5,4},{6,7},{7,6},{8,9},{9,8},{10,11... | collective-permute-start | bytes 786440 | tf_op jit(solution)/shard_map/ppermute | solution.py:302
  46.7 0.0 copy-done.6
  46.7 0.1 constant_dynamic-slice_fusion
  46.8 1.2 %collective-permute-start.18 = (bf16[256,256]{1,0:T(8,128)(2,1)S(1)}, bf16[256,256]{1,0:T(8,128)(2,1)S(1)}, u32[]{:S(2)}, u32[]{:S(2)}) collective-permute-start(bf16[256,256]{1,0:T(8,128)(2,1)S(1)} %get-tuple-element.55), channel_id=1, source_target_pairs={{0,3},{1,2},{2,1},{3,0},{4,7},{5,6},{6,5},{7,4},{8,11},{9,10},{10,... | collective-permute-start | bytes 393224 | tf_op jit(solution)/shard_map/ppermute | solution.py:305
  48.0 0.5 collective-permute-start.17
  48.5 0.0 collective-permute-done.7.rest_3_
  48.5 0.0 collective-permute-done.5.rest_1_
  48.5 2.9 %shard_map.74 = (bf16[512,128]{1,0:T(8,128)(2,1)S(1)}, bf16[512,128]{1,0:T(8,128)(2,1)S(1)}) custom-call(s32[92]{0:T(128)S(1)} %copy-done.1, s32[92]{0:T(128)S(1)} %copy-done.2, s32[320]{0:T(512)S(1)} %copy-done, s32[92]{0:T(128)S(1)} %copy-done.3, s32[92]{0:T(128)S(1)} %copy-done.4, s32[2]{0:T(128)S(1)} %copy-done.5, ...), custom_call_target="tpu_custom_call" | custom-call | tf_op jit(solution)/shard_map/pallas_call | solution.py:365
  51.4 1.6 %collective-permute-start.12 = (bf16[512,128]{1,0:T(8,128)(2,1)S(1)}, bf16[512,128]{1,0:T(8,128)(2,1)S(1)}, u32[]{:S(2)}, u32[]{:S(2)}) collective-permute-start(bf16[512,128]{1,0:T(8,128)(2,1)S(1)} %get-tuple-element.52), channel_id=1, source_target_pairs={{0,2},{1,6},{2,0},{3,4},{4,3},{5,7},{6,1},{7,5},{8,10},{9,14},{10,... | collective-permute-start | bytes 393224 | tf_op jit(solution)/shard_map/ppermute | solution.py:296
  53.0 0.7 collective-permute-start.8
  53.7 0.1 collective-permute-start.13
  53.7 0.0 collective-permute-done.18.refs_11_
  53.7 2.0 %collective-permute-start.9 = (bf16[512,128]{1,0:T(8,128)(2,1)S(1)}, bf16[512,128]{1,0:T(8,128)(2,1)S(1)}, u32[]{:S(2)}, u32[]{:S(2)}) collective-permute-start(bf16[512,128]{1,0:T(8,128)(2,1)S(1)} %get-tuple-element.53), channel_id=1, source_target_pairs={{0,8},{1,12},{2,10},{3,14},{4,9},{5,13},{6,11},{7,15},{8,0},{9,4},... | collective-permute-start | bytes 393224 | tf_op jit(solution)/shard_map/ppermute | solution.py:296
  55.7 0.0 collective-permute-done.17.refs_10_
  55.7 3.0 %collective-permute-start.16 = (bf16[256,256]{1,0:T(8,128)(2,1)S(1)}, bf16[256,256]{1,0:T(8,128)(2,1)S(1)}, u32[]{:S(2)}, u32[]{:S(2)}) collective-permute-start(bf16[256,256]{1,0:T(8,128)(2,1)S(1)} %get-tuple-element.57), channel_id=1, source_target_pairs={{0,1},{1,0},{2,3},{3,2},{4,5},{5,4},{6,7},{7,6},{8,9},{9,8},{10,11... | collective-permute-start | bytes 393224 | tf_op jit(solution)/shard_map/ppermute | solution.py:305
  58.7 0.0 collective-permute-done.12.refs_4_
  58.7 1.2 %collective-permute-start.14 = (bf16[512,128]{1,0:T(8,128)(2,1)S(1)}, bf16[512,128]{1,0:T(8,128)(2,1)S(1)}, u32[]{:S(2)}, u32[]{:S(2)}) collective-permute-start(bf16[512,128]{1,0:T(8,128)(2,1)S(1)} %collective-permute-done.12.refs_4_), channel_id=1, source_target_pairs={{0,1},{1,0},{2,3},{3,2},{4,5},{5,4},{6,7},{7,6},{8,9},{9,8},{10,11... | collective-permute-start | bytes 393224 | tf_op jit(solution)/shard_map/ppermute | solution.py:305
  59.9 0.0 collective-permute-done.8.refs_0_
  59.9 3.9 %collective-permute-start.10 = (bf16[512,128]{1,0:T(8,128)(2,1)S(1)}, bf16[512,128]{1,0:T(8,128)(2,1)S(1)}, u32[]{:S(2)}, u32[]{:S(2)}) collective-permute-start(bf16[512,128]{1,0:T(8,128)(2,1)S(1)} %collective-permute-done.8.refs_0_), channel_id=1, source_target_pairs={{0,1},{1,0},{2,3},{3,2},{4,5},{5,4},{6,7},{7,6},{8,9},{9,8},{10,11... | collective-permute-start | bytes 393224 | tf_op jit(solution)/shard_map/ppermute | solution.py:305
  63.8 0.0 collective-permute-done.13.refs_5_
  63.8 0.0 collective-permute-start.15
  63.8 0.0 collective-permute-done.9.refs_1_
  63.8 0.5 collective-permute-start.11
  64.3 0.0 collective-permute-done.16.refs_9_
  64.4 0.0 collective-permute-done.14.refs_6_
  64.4 0.5 collective-permute-done.10.refs_2_
  64.8 0.4 collective-permute-done.15.refs_7_
  65.2 0.2 collective-permute-done.11.refs_3_
  65.4 1.1 %out_proj.1 = bf16[512,256]{1,0:T(8,128)(2,1)} custom-call(bf16[512,128]{1,0:T(8,128)(2,1)S(1)} %collective-permute-done.8.refs_0_, bf16[512,128]{1,0:T(8,128)(2,1)S(1)} %collective-permute-done.9.refs_1_, bf16[512,128]{1,0:T(8,128)(2,1)S(1)} %collective-permute-done.10.refs_2_, bf16[512,128]{1,0:T(8,128)(2,1)S(1)} %collective-permute-done.11.refs_3_, ...), custom_call_target="tpu_custom_call" | custom-call | tf_op jit(solution)/shard_map/out_proj/pallas_call | solution.py:391
Async XLA Ops:
  3.8 7.7 %collective-permute-start = (bf16[1536,128]{1,0:T(8,128)(2,1)}, bf16[1536,128]{1,0:T(8,128)(2,1)S(1)}, u32[]{:S(2)}, u32[]{:S(2)}) collective-permute-start(bf16[1536,128]{1,0:T(8,128)(2,1)} %get-tuple-element.30), channel_id=1, source_target_pairs={{0,0},{1,4},{2,2},{3,6},{4,1},{5,5},{6,3},{7,7},{8,8},{9,12},{10,1... | collective-permute-start | bytes 1179656 | tf_op jit(solution)/shard_map/ppermute | solution.py:296
  5.5 12.2 %collective-permute-start.3 = (bf16[1536,128]{1,0:T(8,128)(2,1)}, bf16[1536,128]{1,0:T(8,128)(2,1)S(1)}, u32[]{:S(2)}, u32[]{:S(2)}) collective-permute-start(bf16[1536,128]{1,0:T(8,128)(2,1)} %get-tuple-element.45), channel_id=1, source_target_pairs={{0,8},{1,12},{2,10},{3,14},{4,9},{5,13},{6,11},{7,15},{8,0},{9,4},... | collective-permute-start | bytes 1179656 | tf_op jit(solution)/shard_map/ppermute | solution.py:296
  11.5 19.5 %copy-start.4 = (s32[92]{0:T(128)S(1)}, s32[92]{0:T(128)}, u32[]{:S(2)}) copy-start(s32[92]{0:T(128)} %get-tuple-element.41.first) | copy-start | bytes 1108
  11.6 19.5 %copy-start.5 = (s32[2]{0:T(128)S(1)}, s32[2]{0:T(128)}, u32[]{:S(2)}) copy-start(s32[2]{0:T(128)} %get-tuple-element.42.steps) | copy-start | bytes 28
  11.6 19.5 %copy-start = (s32[320]{0:T(512)S(1)}, s32[320]{0:T(512)}, u32[]{:S(2)}) copy-start(s32[320]{0:T(512)} %get-tuple-element.39.which) | copy-start | bytes 3844
  11.6 19.5 %collective-permute-start.2 = (bf16[1536,128]{1,0:T(8,128)(2,1)S(1)}, bf16[1536,128]{1,0:T(8,128)(2,1)S(1)}, u32[]{:S(2)}, u32[]{:S(2)}) collective-permute-start(bf16[1536,128]{1,0:T(8,128)(2,1)S(1)} %collective-permute-done.rest_0_.rest_4_), channel_id=1, source_target_pairs={{0,1},{1,0},{2,3},{3,2},{4,5},{5,4},{6,7},{7,6},{8,9},{9,8},{10,11... | collective-permute-start | bytes 1179656 | tf_op jit(solution)/shard_map/ppermute | solution.py:302
  17.7 13.4 %collective-permute-start.4 = (bf16[1536,128]{1,0:T(8,128)(2,1)S(1)}, bf16[1536,128]{1,0:T(8,128)(2,1)S(1)}, u32[]{:S(2)}, u32[]{:S(2)}) collective-permute-start(bf16[1536,128]{1,0:T(8,128)(2,1)S(1)} %collective-permute-done.3.rest_2_.rest_5_), channel_id=1, source_target_pairs={{0,1},{1,0},{2,3},{3,2},{4,5},{5,4},{6,7},{7,6},{8,9},{9,8},{10,11... | collective-permute-start | bytes 1179656 | tf_op jit(solution)/shard_map/ppermute | solution.py:302
  18.8 12.3 %copy-start.1 = (s32[92]{0:T(128)S(1)}, s32[92]{0:T(128)}, u32[]{:S(2)}) copy-start(s32[92]{0:T(128)} %get-tuple-element.37.who) | copy-start | bytes 1108
  18.8 12.3 %copy-start.2 = (s32[92]{0:T(128)S(1)}, s32[92]{0:T(128)}, u32[]{:S(2)}) copy-start(s32[92]{0:T(128)} %get-tuple-element.38.where) | copy-start | bytes 1108
  18.8 12.3 %copy-start.3 = (s32[92]{0:T(128)S(1)}, s32[92]{0:T(128)}, u32[]{:S(2)}) copy-start(s32[92]{0:T(128)} %get-tuple-element.40.valid) | copy-start | bytes 1108
  18.8 10.4 %collective-permute-start.6 = (bf16[1024,128]{1,0:T(8,128)(2,1)}, bf16[1024,128]{1,0:T(8,128)(2,1)S(1)}, u32[]{:S(2)}, u32[]{:S(2)}) collective-permute-start(bf16[1024,128]{1,0:T(8,128)(2,1)} %get-tuple-element.49), channel_id=1, source_target_pairs={{0,24},{1,28},{2,26},{3,30},{4,25},{5,29},{6,27},{7,31},{8,16},{9,... | collective-permute-start | bytes 786440 | tf_op jit(solution)/shard_map/ppermute | solution.py:296
  22.4 24.3 %copy-start.6 = (bf16[256,1024]{1,0:T(8,128)(2,1)S(1)}, bf16[256,1024]{1,0:T(8,128)(2,1)}, u32[]{:S(2)}) copy-start(bf16[256,1024]{1,0:T(8,128)(2,1)} %param.11) | copy-start | bytes 1572868
  22.4 22.9 %collective-permute-start.1 = (bf16[1024,128]{1,0:T(8,128)(2,1)}, bf16[1024,128]{1,0:T(8,128)(2,1)S(1)}, u32[]{:S(2)}, u32[]{:S(2)}) collective-permute-start(bf16[1024,128]{1,0:T(8,128)(2,1)} %get-tuple-element.43), channel_id=1, source_target_pairs={{0,16},{1,20},{2,18},{3,22},{4,17},{5,21},{6,19},{7,23},{8,24},{9,... | collective-permute-start | bytes 786440 | tf_op jit(solution)/shard_map/ppermute | solution.py:296
  29.2 19.3 %collective-permute-start.7 = (bf16[1024,128]{1,0:T(8,128)(2,1)S(1)}, bf16[1024,128]{1,0:T(8,128)(2,1)S(1)}, u32[]{:S(2)}, u32[]{:S(2)}) collective-permute-start(bf16[1024,128]{1,0:T(8,128)(2,1)S(1)} %collective-permute-done.6.rest_2_), channel_id=1, source_target_pairs={{0,1},{1,0},{2,3},{3,2},{4,5},{5,4},{6,7},{7,6},{8,9},{9,8},{10,11... | collective-permute-start | bytes 786440 | tf_op jit(solution)/shard_map/ppermute | solution.py:302
  45.3 3.2 %collective-permute-start.5 = (bf16[1024,128]{1,0:T(8,128)(2,1)S(1)}, bf16[1024,128]{1,0:T(8,128)(2,1)S(1)}, u32[]{:S(2)}, u32[]{:S(2)}) collective-permute-start(bf16[1024,128]{1,0:T(8,128)(2,1)S(1)} %collective-permute-done.1.rest_0_), channel_id=1, source_target_pairs={{0,1},{1,0},{2,3},{3,2},{4,5},{5,4},{6,7},{7,6},{8,9},{9,8},{10,11... | collective-permute-start | bytes 786440 | tf_op jit(solution)/shard_map/ppermute | solution.py:302
  46.8 6.9 %collective-permute-start.18 = (bf16[256,256]{1,0:T(8,128)(2,1)S(1)}, bf16[256,256]{1,0:T(8,128)(2,1)S(1)}, u32[]{:S(2)}, u32[]{:S(2)}) collective-permute-start(bf16[256,256]{1,0:T(8,128)(2,1)S(1)} %get-tuple-element.55), channel_id=1, source_target_pairs={{0,3},{1,2},{2,1},{3,0},{4,7},{5,6},{6,5},{7,4},{8,11},{9,10},{10,... | collective-permute-start | bytes 393224 | tf_op jit(solution)/shard_map/ppermute | solution.py:305
  48.0 7.8 %collective-permute-start.17 = (bf16[256,256]{1,0:T(8,128)(2,1)S(1)}, bf16[256,256]{1,0:T(8,128)(2,1)S(1)}, u32[]{:S(2)}, u32[]{:S(2)}) collective-permute-start(bf16[256,256]{1,0:T(8,128)(2,1)S(1)} %get-tuple-element.56), channel_id=1, source_target_pairs={{0,2},{1,3},{2,0},{3,1},{4,6},{5,7},{6,4},{7,5},{8,10},{9,11},{10,... | collective-permute-start | bytes 393224 | tf_op jit(solution)/shard_map/ppermute | solution.py:305
  51.4 7.3 %collective-permute-start.12 = (bf16[512,128]{1,0:T(8,128)(2,1)S(1)}, bf16[512,128]{1,0:T(8,128)(2,1)S(1)}, u32[]{:S(2)}, u32[]{:S(2)}) collective-permute-start(bf16[512,128]{1,0:T(8,128)(2,1)S(1)} %get-tuple-element.52), channel_id=1, source_target_pairs={{0,2},{1,6},{2,0},{3,4},{4,3},{5,7},{6,1},{7,5},{8,10},{9,14},{10,... | collective-permute-start | bytes 393224 | tf_op jit(solution)/shard_map/ppermute | solution.py:296
  53.0 6.9 %collective-permute-start.8 = (bf16[512,128]{1,0:T(8,128)(2,1)S(1)}, bf16[512,128]{1,0:T(8,128)(2,1)S(1)}, u32[]{:S(2)}, u32[]{:S(2)}) collective-permute-start(bf16[512,128]{1,0:T(8,128)(2,1)S(1)} %get-tuple-element.52), channel_id=1, source_target_pairs={{0,0},{1,4},{2,2},{3,6},{4,1},{5,5},{6,3},{7,7},{8,8},{9,12},{10,1... | collective-permute-start | bytes 393224 | tf_op jit(solution)/shard_map/ppermute | solution.py:296
  53.7 10.2 %collective-permute-start.13 = (bf16[512,128]{1,0:T(8,128)(2,1)S(1)}, bf16[512,128]{1,0:T(8,128)(2,1)S(1)}, u32[]{:S(2)}, u32[]{:S(2)}) collective-permute-start(bf16[512,128]{1,0:T(8,128)(2,1)S(1)} %get-tuple-element.53), channel_id=1, source_target_pairs={{0,10},{1,14},{2,8},{3,12},{4,11},{5,15},{6,9},{7,13},{8,2},{9,6},... | collective-permute-start | bytes 393224 | tf_op jit(solution)/shard_map/ppermute | solution.py:296
  53.7 10.1 %collective-permute-start.9 = (bf16[512,128]{1,0:T(8,128)(2,1)S(1)}, bf16[512,128]{1,0:T(8,128)(2,1)S(1)}, u32[]{:S(2)}, u32[]{:S(2)}) collective-permute-start(bf16[512,128]{1,0:T(8,128)(2,1)S(1)} %get-tuple-element.53), channel_id=1, source_target_pairs={{0,8},{1,12},{2,10},{3,14},{4,9},{5,13},{6,11},{7,15},{8,0},{9,4},... | collective-permute-start | bytes 393224 | tf_op jit(solution)/shard_map/ppermute | solution.py:296
  55.7 8.6 %collective-permute-start.16 = (bf16[256,256]{1,0:T(8,128)(2,1)S(1)}, bf16[256,256]{1,0:T(8,128)(2,1)S(1)}, u32[]{:S(2)}, u32[]{:S(2)}) collective-permute-start(bf16[256,256]{1,0:T(8,128)(2,1)S(1)} %get-tuple-element.57), channel_id=1, source_target_pairs={{0,1},{1,0},{2,3},{3,2},{4,5},{5,4},{6,7},{7,6},{8,9},{9,8},{10,11... | collective-permute-start | bytes 393224 | tf_op jit(solution)/shard_map/ppermute | solution.py:305
  58.7 5.7 %collective-permute-start.14 = (bf16[512,128]{1,0:T(8,128)(2,1)S(1)}, bf16[512,128]{1,0:T(8,128)(2,1)S(1)}, u32[]{:S(2)}, u32[]{:S(2)}) collective-permute-start(bf16[512,128]{1,0:T(8,128)(2,1)S(1)} %collective-permute-done.12.refs_4_), channel_id=1, source_target_pairs={{0,1},{1,0},{2,3},{3,2},{4,5},{5,4},{6,7},{7,6},{8,9},{9,8},{10,11... | collective-permute-start | bytes 393224 | tf_op jit(solution)/shard_map/ppermute | solution.py:305
  59.9 4.9 %collective-permute-start.10 = (bf16[512,128]{1,0:T(8,128)(2,1)S(1)}, bf16[512,128]{1,0:T(8,128)(2,1)S(1)}, u32[]{:S(2)}, u32[]{:S(2)}) collective-permute-start(bf16[512,128]{1,0:T(8,128)(2,1)S(1)} %collective-permute-done.8.refs_0_), channel_id=1, source_target_pairs={{0,1},{1,0},{2,3},{3,2},{4,5},{5,4},{6,7},{7,6},{8,9},{9,8},{10,11... | collective-permute-start | bytes 393224 | tf_op jit(solution)/shard_map/ppermute | solution.py:305
  63.8 1.3 %collective-permute-start.15 = (bf16[512,128]{1,0:T(8,128)(2,1)S(1)}, bf16[512,128]{1,0:T(8,128)(2,1)S(1)}, u32[]{:S(2)}, u32[]{:S(2)}) collective-permute-start(bf16[512,128]{1,0:T(8,128)(2,1)S(1)} %collective-permute-done.13.refs_5_), channel_id=1, source_target_pairs={{0,1},{1,0},{2,3},{3,2},{4,5},{5,4},{6,7},{7,6},{8,9},{9,8},{10,11... | collective-permute-start | bytes 393224 | tf_op jit(solution)/shard_map/ppermute | solution.py:305
  63.8 1.5 %collective-permute-start.11 = (bf16[512,128]{1,0:T(8,128)(2,1)S(1)}, bf16[512,128]{1,0:T(8,128)(2,1)S(1)}, u32[]{:S(2)}, u32[]{:S(2)}) collective-permute-start(bf16[512,128]{1,0:T(8,128)(2,1)S(1)} %collective-permute-done.9.refs_1_), channel_id=1, source_target_pairs={{0,1},{1,0},{2,3},{3,2},{4,5},{5,4},{6,7},{7,6},{8,9},{9,8},{10,11... | collective-permute-start | bytes 393224 | tf_op jit(solution)/shard_map/ppermute | solution.py:305
